TPU v7x, 256 devices: a whole 4x4x8 slice. The times are simulated.
256 devices in a mesh: row: 16 (over x_lo, y, core), col: 16 (over z, x_hi).
Axes of the slice: x: 4 (x_hi: 2, x_lo: 2; x = x_hi * 2 + x_lo), y: 4, z: 8, core: 2. Of those that a mesh axis runs over, the one named last changes fastest.
Arguments:
- a_panels: bfloat16 [16, 16, 16, 256, 256], P('row', 'col'), may hold values from -1.5 to 1.5
- b_panels: bfloat16 [16, 16, 16, 256, 256], P('row', 'col'), may hold values from -1.5 to 1.5
- a_rows: int32 [16, 16, 16], replicated, may hold values from 0 to 23, as said below
- a_inner: int32 [16, 16, 16], replicated, may hold values from 0 to 23, as said below
- b_inner: int32 [16, 16, 16], replicated, may hold values from 0 to 23, as said below
- b_cols: int32 [16, 16, 16], replicated, may hold values from 0 to 23, as said below
- c_rows: int32 [16, 16, 64], replicated, may hold values from 0 to 23, as said below
- c_cols: int32 [16, 16, 64], replicated, may hold values from 0 to 23
Outputs:
- c_blocks: bfloat16 [16, 16, 64, 256, 256], P('row', 'col')
Inputs may be any that keep to these rules, and one draw needn't show every extreme that they name: `a_rows`: the blocks of one left panel stand at distinct positions; the left blocks and result blocks of one grid row use the same 8 block rows. `a_inner`: all left and right panels draw their inner indices from one common set of 8 indices, which holds 23; every left panel uses 24 - 1. `b_inner`: every right panel holds each index of the common set exactly twice. `b_cols`: the blocks of one right panel stand at distinct positions; the right blocks and result blocks of one grid column use the same 8 block columns. `c_rows`: the 64 result positions of one grid position are distinct and cover every pair of its grid row's block rows and its grid column's block columns.
All inputs are finite; a program needn't handle non-finite values.
Results may differ from a plain program's by a relative error of at most 0.001.
Values may be sent and summed in bfloat16 or wider, within the bound.
A program may use at most 128 MiB of HBM per device.

v0:
```python
import jax
import jax.numpy as jnp
import numpy as np
from jax import lax
from jax.experimental import pallas as pl
from jax.experimental.pallas import tpu as pltpu
from jax.sharding import PartitionSpec as P

STEPS = 4
MESH = pl.DeviceIdType.MESH

BLOCKS = 16
PLUS = 3
MAIN = BLOCKS - PLUS
MAIN_CHUNKS = [(at, min(2, MAIN - at)) for at in range(0, MAIN, 2)]
PLUS_CHUNKS = [(at, 1) for at in range(MAIN, BLOCKS)]
LEFT_CHUNKS = MAIN_CHUNKS + PLUS_CHUNKS
RIGHT_CHUNKS = [(at, 2) for at in range(0, BLOCKS, 2)]
N_MAIN, N_PLUS = len(MAIN_CHUNKS), len(PLUS_CHUNKS)
N_LEFT, N_RIGHT = len(LEFT_CHUNKS), len(RIGHT_CHUNKS)


def place():
    row_id, col_id = lax.axis_index("row"), lax.axis_index("col")
    return row_id // 8, (row_id // 2) % 4, row_id % 2, col_id // 2, col_id % 2


def device(x_lo, y, core, z, x_hi):
    return (x_lo * 8 + y * 2 + core, z * 2 + x_hi)


RUN = 2
RUNS = BLOCKS // RUN
GROUP = 2 * RUN
LAST_ORDER = (0, 1, 2, 3, 4, 5, 7, 6)
PRODUCTS = 2 * STEPS * BLOCKS
NONE = PRODUCTS


def order_table():
    rank = np.zeros(PRODUCTS, np.int32)
    for step in range(STEPS):
        for at in range(RUNS):
            run = LAST_ORDER[at] if step == STEPS - 1 else at
            for n in range(RUN):
                for t in range(2):
                    j = step * 2 * BLOCKS + t * BLOCKS + run * RUN + n
                    rank[j] = (step * RUNS + at) * GROUP + n * 2 + t
    return rank


def fill_tables(rows_ref, inner_ref, b_inner_ref, cols_ref, c_rows_ref, c_cols_ref, rank_row, rank_col, table, last):
    row, col = lax.axis_index("row"), lax.axis_index("col")
    i32 = jnp.int32
    down16 = lax.broadcasted_iota(i32, (BLOCKS, BLOCKS), 0)
    along16 = lax.broadcasted_iota(i32, (BLOCKS, BLOCKS), 1)

    def upright(values):
        spread = jnp.broadcast_to(values, (BLOCKS, BLOCKS))
        return jnp.sum(jnp.where(down16 == along16, spread, 0), axis=1, keepdims=True)

    picks, keys = [], []
    for step in range(STEPS):
        left_col, right_row = (col + step) % 16, (row + step) % 16
        inner = upright(inner_ref[row, pl.ds(left_col, 1), :])
        rows = upright(rows_ref[row, pl.ds(left_col, 1), :])
        b_inner = jnp.broadcast_to(b_inner_ref[right_row, pl.ds(col, 1), :], (BLOCKS, BLOCKS))
        b_cols = jnp.broadcast_to(cols_ref[right_row, pl.ds(col, 1), :], (BLOCKS, BLOCKS))
        match = inner == b_inner
        first = jnp.min(jnp.where(match, along16, BLOCKS), axis=1, keepdims=True)
        second = jnp.min(jnp.where(match & (along16 > first), along16, BLOCKS), axis=1, keepdims=True)
        for pick in (first, second):
            cols = jnp.sum(jnp.where(along16 == pick, b_cols, 0), axis=1, keepdims=True)
            picks.append(jnp.minimum(pick, BLOCKS - 1))
            keys.append(rows * 32 + cols)
    pick_col, key_col = jnp.concatenate(picks, axis=0), jnp.concatenate(keys, axis=0)
    square = (PRODUCTS, PRODUCTS)
    eye = lax.broadcasted_iota(i32, square, 0) == lax.broadcasted_iota(i32, square, 1)

    def level(values):
        return jnp.sum(jnp.where(eye, jnp.broadcast_to(values, square), 0), axis=0, keepdims=True)

    key_row = level(key_col)
    ranks = jnp.broadcast_to(rank_col[...], square)
    earlier = (jnp.broadcast_to(key_col, square) == key_row) & (ranks < rank_row[...])
    before = jnp.max(jnp.where(earlier, ranks, -1), axis=0, keepdims=True)
    table[0:1, :] = level(pick_col)
    table[1:2, :] = jnp.where(before < 0, NONE, before)
    slots = c_rows_ref.shape[2]
    slot_key = c_rows_ref[row, pl.ds(col, 1), :] * 32 + c_cols_ref[row, pl.ds(col, 1), :]
    tall = (PRODUCTS, slots)
    landed = jnp.broadcast_to(key_col, tall) == slot_key
    final = jnp.max(jnp.where(landed, jnp.broadcast_to(rank_col[...], tall), -1), axis=0, keepdims=True)
    last[...] = jnp.where(final < 0, NONE, final)


def gather_kernel(a_ref, b_ref, rows_ref, inner_ref, b_inner_ref, cols_ref, c_rows_ref, c_cols_ref, rank_row, rank_col,
                  partial, last,
                  a_own, b_own, j1, j2, j3, i1, i2, i3, q3, q6, relay, sums, stage, table, plain,
                  own_sem, table_sem, stage_sem,
                  s_j1, s_j2, s_j3, s_i1, s_i2, s_i2b, s_i3, s_q3, s_q6, s_rl, s_fw,
                  r_j1, r_j2, r_j3, r_i1, r_i2, r_i3, r_q3, r_q6, r_rl):
    x_lo, y, core, z, x_hi = place()
    own = a_ref.at[0, 0]
    own_b = b_ref.at[0, 0]
    even = y % 2 == 0
    wraps1 = (3 - y) // 3
    wraps2 = 1 - y // 2
    down = device(x_lo, y, core, (z + 7) % 8, x_hi)
    up = device(x_lo, y, core, (z + 1) % 8, x_hi)
    up3 = device(x_lo, y, core, (z + 3) % 8, x_hi)
    down3 = device(x_lo, y, core, (z + 5) % 8, x_hi)
    across = device(x_lo, y, core, z, 1 - x_hi)
    twin = device(x_lo, y, 1 - core, z, x_hi)
    prev1 = device((x_lo + wraps1) % 2, (y + 3) % 4, core, z, x_hi)
    after1 = device((x_lo + y // 3) % 2, (y + 1) % 4, core, z, x_hi)
    prev2 = device((x_lo + wraps2) % 2, (y + 2) % 4, 1 - core, z, x_hi)
    after2 = device((x_lo + y // 2) % 2, (y + 2) % 4, 1 - core, z, x_hi)
    wrap = device(x_lo, (y + 3) % 4, core, z, x_hi)
    next_y = device(x_lo, (y + 1) % 4, core, z, x_hi)
    beside = device(1 - x_lo, y, core, z, x_hi)

    barrier = pltpu.get_barrier_semaphore()
    others = (down, up, up3, down3, across, twin, prev1, after1, prev2, after2, wrap, next_y, beside)
    for other in others:
        pl.semaphore_signal(barrier, inc=1, device_id=other, device_id_type=MESH)
    pl.semaphore_wait(barrier, len(others))

    take_own = [
        pltpu.make_async_copy(own, a_own, own_sem.at[0]),
        pltpu.make_async_copy(own_b, b_own, own_sem.at[1]),
    ]

    def part(ref, chunk, shift=0):
        return ref.at[pl.ds(chunk[0] - shift, chunk[1])]

    def send(src, dst, s_sem, r_sem, to):
        return pltpu.make_async_remote_copy(
            src_ref=src, dst_ref=dst, send_sem=s_sem, recv_sem=r_sem, device_id=to, device_id_type=MESH
        )

    def to_j2(k, src, to):
        return send(src, part(j2, LEFT_CHUNKS[k]), s_j2.at[k], r_j2.at[k], to)

    def to_j1(k, src):
        return send(part(src, LEFT_CHUNKS[k]), part(j1, LEFT_CHUNKS[k]), s_j1.at[k], r_j1.at[k], across)

    def to_j3(k, src, to):
        return send(src, part(j3, LEFT_CHUNKS[k]), s_j3.at[k], r_j3.at[k], to)

    def to_q3(k):
        chunk = PLUS_CHUNKS[k]
        return send(part(own, chunk), part(q3, chunk, MAIN), s_q3.at[k], r_q3.at[k], up3)

    def to_q6(k):
        chunk = PLUS_CHUNKS[k]
        return send(part(q3, chunk, MAIN), part(q6, chunk, MAIN), s_q6.at[k], r_q6.at[k], up3)

    def to_right(k, src, dst, s_sem, r_sem, to):
        return send(part(src, RIGHT_CHUNKS[k]), part(dst, RIGHT_CHUNKS[k]), s_sem.at[k], r_sem.at[k], to)

    for k in range(N_PLUS):
        to_q3(k).start()
    for k in range(max(N_MAIN, N_RIGHT)):
        if k < N_MAIN:
            to_j2(k, part(own, LEFT_CHUNKS[k]), down).start()

            @pl.when(x_hi == 1)
            def _():
                to_j1(k, own).start()

        if k < N_RIGHT:

            @pl.when(core == 0)
            def _():
                @pl.when(y % 2 == 1)
                def _():
                    to_right(k, own_b, i2, s_i2b, r_i2, prev1).start()

                @pl.when(y % 2 == 0)
                def _():
                    to_right(k, own_b, i3, s_i3, r_i3, prev2).start()

            @pl.when(core == 1)
            def _():
                to_right(k, own_b, i1, s_i1, r_i1, twin).start()

                @pl.when(y == 0)
                def _():
                    to_right(k, own_b, relay, s_rl, r_rl, wrap).start()

                @pl.when(y != 0)
                def _():
                    to_right(k, own_b, i2, s_i2, r_i2, prev1).start()

    @pl.when(x_hi == 1)
    def _():
        for k in range(N_MAIN, N_LEFT):
            to_j1(k, own).start()

    @pl.when((core == 0) & (y % 2 == 1))
    def _():
        for k in range(N_RIGHT):
            to_right(k, own_b, i3, s_i3, r_i3, prev2).start()

    for copy in take_own:
        copy.start()
    fill_tables(rows_ref, inner_ref, b_inner_ref, cols_ref, c_rows_ref, c_cols_ref, rank_row, rank_col, table, last)
    to_plain = pltpu.make_async_copy(table, plain, table_sem)
    to_plain.start()
    sums[NONE] = jnp.zeros(sums.shape[1:], sums.dtype)
    stage[...] = jnp.zeros(stage.shape, stage.dtype)

    def put(group):
        return pltpu.make_async_copy(
            stage.at[group % 2], partial.at[pl.ds(group * GROUP, GROUP)], stage_sem.at[group % 2]
        )

    for n in range(2):
        put(PRODUCTS // GROUP + n).start()
    to_plain.wait()

    def on_j2(k):
        to_j2(k, part(own, LEFT_CHUNKS[k]), down).wait_recv()

        @pl.when(x_hi == 0)
        def _():
            to_j1(k, j2).start()

        if k >= N_MAIN:

            @pl.when(x_hi == 1)
            def _():
                to_j3(k, part(j2, LEFT_CHUNKS[k]), across).start()

    def on_j1(k):
        to_j1(k, own).wait_recv()
        if k < N_MAIN:
            to_j3(k, part(j1, LEFT_CHUNKS[k]), down).start()

    def on_j3(k):
        to_j3(k, part(j1, LEFT_CHUNKS[k]), down).wait_recv()

    def on_q3(k):
        to_q3(k).wait_recv()
        to_q6(k).start()

    def on_q6(k):
        to_q6(k).wait_recv()
        mine = part(q6, PLUS_CHUNKS[k], MAIN)
        to_j2(N_MAIN + k, mine, up).start()

        @pl.when(x_hi == 0)
        def _():
            to_j3(N_MAIN + k, mine, across).start()

    def on_i1(k):
        to_right(k, own_b, i1, s_i1, r_i1, twin).wait_recv()

        @pl.when((core == 1) & (y % 2 == 1))
        def _():
            to_right(k, i1, i2, s_i2b, r_i2, twin).start()

    def on_i2(k):
        to_right(k, own_b, i2, s_i2, r_i2, prev1).wait_recv()

        @pl.when(core == 1)
        def _():
            to_right(k, i2, i3, s_i3, r_i3, twin).start()

        @pl.when((core == 0) & (y % 2 == 0))
        def _():
            to_right(k, i2, i1, s_i1, r_i1, twin).start()

    def on_i3(k):
        to_right(k, own_b, i3, s_i3, r_i3, prev2).wait_recv()

        @pl.when((core == 1) & (y % 2 == 0))
        def _():
            to_right(k, i3, i1, s_fw, r_i1, next_y).start()

    def on_relay(k):
        @pl.when((core == 1) & (y == 3))
        def _():
            to_right(k, own_b, relay, s_rl, r_rl, wrap).wait_recv()
            to_right(k, relay, i2, s_fw, r_i2, beside).start()

    lefts, rights = (a_own, j1, j2, j3), (b_own, i1, i2, i3)

    def multiply_run(step, run, group):
        put(group).wait()
        for n in range(RUN):
            block = lefts[step][run * RUN + n]
            for t in range(2):
                j = step * 2 * BLOCKS + t * BLOCKS + run * RUN + n
                rank = group * GROUP + 2 * n + t
                total = sums[plain[1, j]] + jnp.dot(
                    block, rights[step][plain[0, j]], preferred_element_type=jnp.float32
                )
                sums[rank] = total
                stage[group % 2, 2 * n + t] = total.astype(stage.dtype)
        put(group).start()

    def multiply(step, first, count):
        if count == 1:
            run = LAST_ORDER[first] if step == STEPS - 1 else first
            multiply_run(step, run, step * RUNS + first)
        else:

            @pl.loop(first, first + count)
            def _(run):
                multiply_run(step, run, step * RUNS + run)

    for event in schedule():
        kind, arg = event[0], event[1:]
        if kind == "own":
            for copy in take_own:
                copy.wait()
        elif kind == "x":
            multiply(*arg)
        else:
            {"j1": on_j1, "j2": on_j2, "j3": on_j3, "q3": on_q3, "q6": on_q6,
             "i1": on_i1, "i2": on_i2, "i3": on_i3, "rl": on_relay}[kind](*arg)
    for group in range(2):
        put(group).wait()

    for k in range(N_LEFT):
        chunk = LEFT_CHUNKS[k]
        to_j2(k, part(own, chunk), down).wait_send()
        to_j1(k, own).wait_send()
        to_j3(k, part(own, chunk), down).wait_send()
    for k in range(N_PLUS):
        to_q3(k).wait_send()
        to_q6(k).wait_send()
    for k in range(N_RIGHT):
        to_right(k, own_b, i3, s_i3, r_i3, twin).wait_send()

        @pl.when((core == 1) | even)
        def _():
            to_right(k, own_b, i1, s_i1, r_i1, twin).wait_send()

        @pl.when(y % 2 == 1)
        def _():
            to_right(k, own_b, i2, s_i2b, r_i2, twin).wait_send()

        @pl.when((core == 1) & (y != 0))
        def _():
            to_right(k, own_b, i2, s_i2, r_i2, prev1).wait_send()

        @pl.when((core == 1) & (y != 1))
        def _():
            to_right(k, own_b, i1, s_fw, r_i1, next_y).wait_send()

        @pl.when((core == 1) & (y == 0))
        def _():
            to_right(k, own_b, relay, s_rl, r_rl, wrap).wait_send()


def schedule():
    timed = [(1, "own"), (4.5, "x", 0, 0, RUNS)]
    for k in range(N_MAIN):
        timed += [(5.4 * (k + 1) + 2, "j2", k), (16 + 5.4 * (k + 1), "j1", k), (46 + 5 * (k + 1), "j3", k)]
    for k in range(N_PLUS):
        timed += [
            (8.6 * (k + 1) + 2, "q3", k),
            (12 + 17 * (k + 1), "q6", k),
            (18 + 17 * (k + 1), "j2", N_MAIN + k),
            (24 + 17 * (k + 1), "j1", N_MAIN + k),
            (75 + k, "j3", N_MAIN + k),
        ]
    for k in range(N_RIGHT):
        timed += [
            (5.5 * (k + 1) + 2, "rl", k),
            (8.5 * (k + 1) + 2, "i3", k),
            (56 + 0.1 * k, "i2", k),
            (59 + 0.1 * k, "i1", k),
        ]
    timed.sort(key=lambda event: event[0])
    events = [event[1:] for event in timed]
    todo = [(1, 0, RUNS), (2, 0, RUNS), (3, 0, 4), (3, 4, 1), (3, 5, 1), (3, 6, 1), (3, 7, 1)]
    done, out = set(), []

    def needs(step, first, count):
        places = range(first, first + count)
        runs = [LAST_ORDER[at] if step == STEPS - 1 else at for at in places]
        blocks = {run * RUN + n for run in runs for n in range(RUN)}
        chunks = {k for k, (at, n) in enumerate(LEFT_CHUNKS) if blocks & set(range(at, at + n))}
        return {(f"j{step}", k) for k in chunks} | {(f"i{step}", k) for k in range(N_RIGHT)}

    for event in events:
        out.append(event)
        done.add(event)
        while todo and needs(*todo[0]) <= done:
            out.append(("x", *todo.pop(0)))
    return out


def gather(a_panels, b_panels, indices):
    dtype = a_panels.dtype
    tail = a_panels.shape[3:]
    slots = indices[-1].shape[2]
    rank = order_table()
    anywhere = pl.BlockSpec(memory_space=pl.ANY)
    in_vmem = pl.BlockSpec(memory_space=pltpu.VMEM)
    sems = [2, 1, 2]
    sems += [N_LEFT] * 3 + [N_RIGHT] * 4 + [N_PLUS] * 2 + [N_RIGHT] * 2
    sems += [N_LEFT] * 3 + [N_RIGHT] * 3 + [N_PLUS] * 2 + [N_RIGHT]
    scratch = [pltpu.VMEM((BLOCKS, *tail), dtype)] * 8 + [pltpu.VMEM((PLUS, *tail), dtype)] * 2
    scratch += [
        pltpu.VMEM((BLOCKS, *tail), dtype),
        pltpu.VMEM((PRODUCTS + 1, *tail), jnp.float32),
        pltpu.VMEM((2, GROUP, *tail), dtype),
        pltpu.VMEM((8, PRODUCTS), jnp.int32),
        pltpu.SMEM((8, PRODUCTS), jnp.int32),
    ]
    return pl.pallas_call(
        gather_kernel,
        out_shape=[
            jax.ShapeDtypeStruct((PRODUCTS + 2 * GROUP, *tail), dtype),
            jax.ShapeDtypeStruct((1, slots), jnp.int32),
        ],
        in_specs=[anywhere] * 2 + [in_vmem] * 8,
        out_specs=[anywhere, in_vmem],
        scratch_shapes=scratch + [pltpu.SemaphoreType.DMA((n,)) if n > 1 else pltpu.SemaphoreType.DMA for n in sems],
        compiler_params=pltpu.CompilerParams(collective_id=0, has_side_effects=True, vmem_limit_bytes=67000000),
        name="gather",
    )(a_panels, b_panels, *indices, jnp.asarray(rank)[None, :], jnp.asarray(rank)[:, None])


def place_kernel(last, partial, out, stage, in_sem, out_sem):
    count = stage.shape[0]

    def fetch(n):
        return pltpu.make_async_copy(partial.at[last[0, n]], stage.at[n], in_sem.at[n])

    def put(n):
        return pltpu.make_async_copy(stage.at[n], out.at[0, 0, n], out_sem.at[n])

    @pl.loop(0, count)
    def _(n):
        fetch(n).start()

    @pl.loop(0, count)
    def _(n):
        fetch(n).wait()
        put(n).start()

    @pl.loop(0, count)
    def _(n):
        put(n).wait()


def on_device(a_panels, b_panels, a_rows, a_inner, b_inner, b_cols, c_rows, c_cols):
    partial, last = gather(a_panels, b_panels, (a_rows, a_inner, b_inner, b_cols, c_rows, c_cols))
    slots, width = c_rows.shape[2], a_panels.shape[3]
    anywhere = pl.BlockSpec(memory_space=pl.ANY)
    return pl.pallas_call(
        place_kernel,
        out_shape=jax.ShapeDtypeStruct((1, 1, slots, width, width), a_panels.dtype),
        grid_spec=pltpu.PrefetchScalarGridSpec(
            num_scalar_prefetch=1,
            grid=(),
            in_specs=[anywhere],
            out_specs=anywhere,
            scratch_shapes=[
                pltpu.VMEM((slots, width, width), a_panels.dtype),
                pltpu.SemaphoreType.DMA((slots,)),
                pltpu.SemaphoreType.DMA((slots,)),
            ],
        ),
        name="place",
    )(last, partial)


def solution(mesh):
    in_specs = (
        P("row", "col", None, None, None),
        P("row", "col", None, None, None),
        P(),
        P(),
        P(),
        P(),
        P(),
        P(),
    )
    out_specs = P("row", "col", None, None, None)
    return jax.shard_map(
        on_device, mesh=mesh, in_specs=in_specs, out_specs=out_specs, check_vma=False
    )
```

profile of v0, /device:TPU:30, one launch (start us, length us, event | category | flops | bytes accessed | tf_op | source)
XLA Modules:
  0.0 134.6 jit_solution(2053500662966691984)
XLA Ops:
  0.0 125.7 %gather.1 = (bf16[136,256,256]{2,1,0:T(8,128)(2,1)}, s32[1,64]{1,0:T(1,128)}) custom-call(bf16[1,1,16,256,256]{4,3,2,1,0:T(8,128)(2,1)} %a_ref.1, bf16[1,1,16,256,256]{4,3,2,1,0:T(8,128)(2,1)} %b_ref.1, s32[16,16,16]{2,1,0:T(8,128)} %rows_ref.1, s32[16,16,16]{2,1,0:T(8,128)} %inner_ref.1, s32[16,16,16]{2,1,0:T(8,128)} %b_inner_ref.1, ...), custom_call_target="tpu_custom_call" | custom-call | tf_op jit(solution)/shard_map/gather/pallas_call | solution.py:416
  125.7 8.9 %place.1 = bf16[1,1,64,256,256]{4,3,2,1,0:T(8,128)(2,1)} custom-call(s32[1,64]{1,0:T(1,128)} %get-tuple-element.7.last, bf16[136,256,256]{2,1,0:T(8,128)(2,1)} %get-tuple-element.8.partial), custom_call_target="tpu_custom_call" | custom-call | tf_op jit(solution)/shard_map/place/pallas_call | solution.py:457
where the time goes:
time: 135 us
  Pallas kernels  135 us (100%)
    pallas_call x1, Pallas kernels, gather(): pl.pallas_call(gather_kernel, out_shape=[jax.ShapeDtypeStruct((PRODUCTS +...  126 us
    pallas_call x1, Pallas kernels, on_device(): pl.pallas_call(place_kernel, out_shape=jax.ShapeDtypeStruct((1, 1, slots,...  8.86 us

commit v1 on v0

--- a/solution.py
+++ b/solution.py
@@ -29,23 +29,36 @@
     return (x_lo * 8 + y * 2 + core, z * 2 + x_hi)
 
 
+LEAD = 1
+CROSS_AT = (-1, -1, -1, 3)
+HALF = N_RIGHT // 2
 RUN = 2
 RUNS = BLOCKS // RUN
 GROUP = 2 * RUN
-LAST_ORDER = (0, 1, 2, 3, 4, 5, 7, 6)
 PRODUCTS = 2 * STEPS * BLOCKS
 NONE = PRODUCTS
+PIECES = ((0, 0, RUNS), (1, 0, 6), (3, 0, 2), (2, 0, 6), (3, 4, 1), (3, 3, 1), (3, 2, 1), (2, 6, 1), (2, 7, 1), (3, 5, 1), (1, 6, 1), (1, 7, 1), (3, 6, 1), (3, 7, 1))
+ORDERS = (
+(
+    ("rl", 0), ("j2", 0), ("rl", 4), ("j1", 0), ("q3", 0), ("rl", 5), ("j2", 1), ("q3", 1), ("rl", 1), ("rl", 7),
+    ("rl", 6), ("j2", 2), ("q3", 2), ("j1", 2), ("j2", 3), ("rl", 2), ("i2", 0), ("rl", 3), ("j2", 4), ("j1", 1),
+    ("i2", 1), ("j2", 5), ("i3", 0), ("i1", 0), ("j2", 6), ("j1", 3), ("i2", 5), ("i2", 4), ("i3", 1), ("i1", 1),
+    ("i3", 4), ("i1", 4), ("q6", 1), ("q6", 0), ("j1", 4), ("q6", 2), ("i2", 6), ("i3", 5), ("i1", 5), ("j2", 8),
+    ("j3", 1), ("i2", 7), ("i2", 2), ("i3", 2), ("i1", 2), ("j2", 7), ("i3", 6), ("i1", 6), ("i2", 3), ("j3", 0),
+    ("i3", 7), ("i1", 7), ("j2", 9), ("j1", 5), ("j1", 6), ("j3", 2), ("i3", 3), ("i1", 3), ("j3", 3), ("j3", 4),
+    ("j1", 7), ("j3", 7), ("j3", 5), ("j1", 8), ("j3", 8), ("j3", 6), ("j1", 9), ("j3", 9),
+),
+)
 
 
 def order_table():
     rank = np.zeros(PRODUCTS, np.int32)
-    for step in range(STEPS):
-        for at in range(RUNS):
-            run = LAST_ORDER[at] if step == STEPS - 1 else at
-            for n in range(RUN):
-                for t in range(2):
-                    j = step * 2 * BLOCKS + t * BLOCKS + run * RUN + n
-                    rank[j] = (step * RUNS + at) * GROUP + n * 2 + t
+    at = 0
+    for step, first, count in PIECES:
+        for block in range(first * RUN, (first + count) * RUN):
+            for t in range(2):
+                rank[step * 2 * BLOCKS + t * BLOCKS + block] = at
+                at += 1
     return rank
 
 
@@ -98,7 +111,7 @@
                   partial, last,
                   a_own, b_own, j1, j2, j3, i1, i2, i3, q3, q6, relay, sums, stage, table, plain,
                   own_sem, table_sem, stage_sem,
-                  s_j1, s_j2, s_j3, s_i1, s_i2, s_i2b, s_i3, s_q3, s_q6, s_rl, s_fw,
+                  s_j1, s_j2, s_j3, s_i1, s_i2, s_i2b, s_i3, s_q3, s_q6, s_rl, s_fw, s_x,
                   r_j1, r_j2, r_j3, r_i1, r_i2, r_i3, r_q3, r_q6, r_rl):
     x_lo, y, core, z, x_hi = place()
     own = a_ref.at[0, 0]
@@ -121,7 +134,16 @@
     beside = device(1 - x_lo, y, core, z, x_hi)
 
     barrier = pltpu.get_barrier_semaphore()
-    others = (down, up, up3, down3, across, twin, prev1, after1, prev2, after2, wrap, next_y, beside)
+    apart = device(x_lo, (y + 2) % 4, 1 - core, z, x_hi)
+    beside_twin = device(1 - x_lo, y, 1 - core, z, x_hi)
+    wrap_twin = device(x_lo, (y + 3) % 4, 1 - core, z, x_hi)
+    next_twin = device(x_lo, (y + 1) % 4, 1 - core, z, x_hi)
+    prev2_same = device((x_lo + wraps2) % 2, (y + 2) % 4, core, z, x_hi)
+    after2_same = device((x_lo + y // 2) % 2, (y + 2) % 4, core, z, x_hi)
+    others = (
+        down, up, up3, down3, across, twin, prev1, after1, prev2, after2, wrap, next_y, beside,
+        apart, beside_twin, wrap_twin, next_twin, prev2_same, after2_same,
+    )
     for other in others:
         pl.semaphore_signal(barrier, inc=1, device_id=other, device_id_type=MESH)
     pl.semaphore_wait(barrier, len(others))
@@ -158,12 +180,22 @@
 
     def to_right(k, src, dst, s_sem, r_sem, to):
         return send(part(src, RIGHT_CHUNKS[k]), part(dst, RIGHT_CHUNKS[k]), s_sem.at[k], r_sem.at[k], to)
+
+    def cross(k):
+        @pl.when((core == 0) & (y == 0))
+        def _():
+            to_right(k, own_b, i3, s_i3, r_i3, prev2).start()
+
+        @pl.when((core == 0) & (y == 1))
+        def _():
+            to_right(k, own_b, relay, s_rl, r_rl, beside).start()
 
     for k in range(N_PLUS):
         to_q3(k).start()
     for k in range(max(N_MAIN, N_RIGHT)):
         if k < N_MAIN:
             to_j2(k, part(own, LEFT_CHUNKS[k]), down).start()
+        if k < LEAD:
 
             @pl.when(x_hi == 1)
             def _():
@@ -177,31 +209,36 @@
                 def _():
                     to_right(k, own_b, i2, s_i2b, r_i2, prev1).start()
 
-                @pl.when(y % 2 == 0)
+                @pl.when(y == 2)
                 def _():
                     to_right(k, own_b, i3, s_i3, r_i3, prev2).start()
 
+                if k >= HALF:
+
+                    @pl.when(y < 2)
+                    def _():
+                        to_right(k, own_b, relay, s_rl, r_rl, twin).start()
+
             @pl.when(core == 1)
             def _():
                 to_right(k, own_b, i1, s_i1, r_i1, twin).start()
 
                 @pl.when(y == 0)
                 def _():
-                    to_right(k, own_b, relay, s_rl, r_rl, wrap).start()
+                    to_right(k, own_b, relay, s_rl, r_rl, wrap if k < HALF else wrap_twin).start()
 
                 @pl.when(y != 0)
                 def _():
                     to_right(k, own_b, i2, s_i2, r_i2, prev1).start()
 
-    @pl.when(x_hi == 1)
-    def _():
-        for k in range(N_MAIN, N_LEFT):
-            to_j1(k, own).start()
-
-    @pl.when((core == 0) & (y % 2 == 1))
+    @pl.when((core == 0) & (y == 3))
     def _():
         for k in range(N_RIGHT):
             to_right(k, own_b, i3, s_i3, r_i3, prev2).start()
+
+    for k in range(HALF):
+        if CROSS_AT[k] < 0:
+            cross(k)
 
     for copy in take_own:
         copy.start()
@@ -227,11 +264,21 @@
         def _():
             to_j1(k, j2).start()
 
+        if k + LEAD < N_LEFT:
+
+            @pl.when(x_hi == 1)
+            def _():
+                to_j1(k + LEAD, own).start()
+
         if k >= N_MAIN:
 
             @pl.when(x_hi == 1)
             def _():
                 to_j3(k, part(j2, LEFT_CHUNKS[k]), across).start()
+
+        for n in range(HALF):
+            if CROSS_AT[n] == k:
+                cross(n)
 
     def on_j1(k):
         to_j1(k, own).wait_recv()
@@ -280,10 +327,28 @@
             to_right(k, i3, i1, s_fw, r_i1, next_y).start()
 
     def on_relay(k):
-        @pl.when((core == 1) & (y == 3))
-        def _():
-            to_right(k, own_b, relay, s_rl, r_rl, wrap).wait_recv()
-            to_right(k, relay, i2, s_fw, r_i2, beside).start()
+        arrived = to_right(k, own_b, relay, s_rl, r_rl, wrap)
+        if k >= HALF:
+
+            @pl.when((core == 1) & (y == 0))
+            def _():
+                arrived.wait_recv()
+                to_right(k, relay, i3, s_x, r_i3, prev2_same).start()
+
+            @pl.when((core == 1) & (y == 1))
+            def _():
+                arrived.wait_recv()
+                to_right(k, relay, relay, s_x, r_rl, beside_twin).start()
+
+        @pl.when((core == 0) & (y == 1))
+        def _():
+            arrived.wait_recv()
+            to_right(k, relay, i3, s_i3, r_i3, apart).start()
+
+        @pl.when((core == (1 if k < HALF else 0)) & (y == 3))
+        def _():
+            arrived.wait_recv()
+            to_right(k, relay, i2, s_x, r_i2, beside if k < HALF else beside_twin).start()
 
     lefts, rights = (a_own, j1, j2, j3), (b_own, i1, i2, i3)
 
@@ -301,26 +366,40 @@
                 stage[group % 2, 2 * n + t] = total.astype(stage.dtype)
         put(group).start()
 
-    def multiply(step, first, count):
+    def multiply(step, first, count, group):
         if count == 1:
-            run = LAST_ORDER[first] if step == STEPS - 1 else first
-            multiply_run(step, run, step * RUNS + first)
+            multiply_run(step, first, group)
         else:
 
-            @pl.loop(first, first + count)
-            def _(run):
-                multiply_run(step, run, step * RUNS + run)
-
-    for event in schedule():
-        kind, arg = event[0], event[1:]
-        if kind == "own":
-            for copy in take_own:
-                copy.wait()
-        elif kind == "x":
-            multiply(*arg)
-        else:
-            {"j1": on_j1, "j2": on_j2, "j3": on_j3, "q3": on_q3, "q6": on_q6,
-             "i1": on_i1, "i2": on_i2, "i3": on_i3, "rl": on_relay}[kind](*arg)
+            @pl.loop(0, count)
+            def _(n):
+                multiply_run(step, first + n, group + n)
+
+    handlers = {
+        "j1": on_j1, "j2": on_j2, "j3": on_j3, "q3": on_q3, "q6": on_q6,
+        "i1": on_i1, "i2": on_i2, "i3": on_i3, "rl": on_relay,
+    }
+
+    for copy in take_own:
+        copy.wait()
+    multiply(*PIECES[0], 0)
+
+    def follow(order):
+        for event in with_products(order):
+            if event[0] == "x":
+                multiply(*event[1:])
+            else:
+                handlers[event[0]](event[1])
+
+    if len(ORDERS) == 1:
+        follow(ORDERS[0])
+    else:
+        for which, order in enumerate(ORDERS):
+
+            @pl.when(core == which)
+            def _():
+                follow(order)
+
     for group in range(2):
         put(group).wait()
 
@@ -333,7 +412,11 @@
         to_q3(k).wait_send()
         to_q6(k).wait_send()
     for k in range(N_RIGHT):
-        to_right(k, own_b, i3, s_i3, r_i3, twin).wait_send()
+        first_half = k < HALF
+
+        @pl.when((core == 1) | (y != 0) | first_half)
+        def _():
+            to_right(k, own_b, i3, s_i3, r_i3, twin).wait_send()
 
         @pl.when((core == 1) | even)
         def _():
@@ -347,51 +430,39 @@
         def _():
             to_right(k, own_b, i2, s_i2, r_i2, prev1).wait_send()
 
-        @pl.when((core == 1) & (y != 1))
+        @pl.when((core == 1) & even)
         def _():
             to_right(k, own_b, i1, s_fw, r_i1, next_y).wait_send()
 
-        @pl.when((core == 1) & (y == 0))
+        if first_half:
+            staged, passed = ((core == 0) & (y == 1)) | ((core == 1) & (y == 0)), (core == 1) & (y == 3)
+        else:
+            staged = ((core == 0) & (y < 2)) | ((core == 1) & (y == 0))
+            passed = ((core == 1) & (y < 2)) | ((core == 0) & (y == 3))
+
+        @pl.when(staged)
         def _():
             to_right(k, own_b, relay, s_rl, r_rl, wrap).wait_send()
 
-
-def schedule():
-    timed = [(1, "own"), (4.5, "x", 0, 0, RUNS)]
-    for k in range(N_MAIN):
-        timed += [(5.4 * (k + 1) + 2, "j2", k), (16 + 5.4 * (k + 1), "j1", k), (46 + 5 * (k + 1), "j3", k)]
-    for k in range(N_PLUS):
-        timed += [
-            (8.6 * (k + 1) + 2, "q3", k),
-            (12 + 17 * (k + 1), "q6", k),
-            (18 + 17 * (k + 1), "j2", N_MAIN + k),
-            (24 + 17 * (k + 1), "j1", N_MAIN + k),
-            (75 + k, "j3", N_MAIN + k),
-        ]
-    for k in range(N_RIGHT):
-        timed += [
-            (5.5 * (k + 1) + 2, "rl", k),
-            (8.5 * (k + 1) + 2, "i3", k),
-            (56 + 0.1 * k, "i2", k),
-            (59 + 0.1 * k, "i1", k),
-        ]
-    timed.sort(key=lambda event: event[0])
-    events = [event[1:] for event in timed]
-    todo = [(1, 0, RUNS), (2, 0, RUNS), (3, 0, 4), (3, 4, 1), (3, 5, 1), (3, 6, 1), (3, 7, 1)]
+        @pl.when(passed)
+        def _():
+            to_right(k, own_b, relay, s_x, r_rl, wrap).wait_send()
+
+
+def with_products(order):
+    todo, group = [], RUNS
+    for step, first, count in PIECES[1:]:
+        blocks = set(range(first * RUN, (first + count) * RUN))
+        chunks = {k for k, (at, n) in enumerate(LEFT_CHUNKS) if blocks & set(range(at, at + n))}
+        needs = {(f"j{step}", k) for k in chunks} | {(f"i{step}", k) for k in range(N_RIGHT)}
+        todo.append((needs, ("x", step, first, count, group)))
+        group += count
     done, out = set(), []
-
-    def needs(step, first, count):
-        places = range(first, first + count)
-        runs = [LAST_ORDER[at] if step == STEPS - 1 else at for at in places]
-        blocks = {run * RUN + n for run in runs for n in range(RUN)}
-        chunks = {k for k, (at, n) in enumerate(LEFT_CHUNKS) if blocks & set(range(at, at + n))}
-        return {(f"j{step}", k) for k in chunks} | {(f"i{step}", k) for k in range(N_RIGHT)}
-
-    for event in events:
+    for event in order:
         out.append(event)
         done.add(event)
-        while todo and needs(*todo[0]) <= done:
-            out.append(("x", *todo.pop(0)))
+        while todo and todo[0][0] <= done:
+            out.append(todo.pop(0)[1])
     return out
 
 
@@ -403,7 +474,7 @@
     anywhere = pl.BlockSpec(memory_space=pl.ANY)
     in_vmem = pl.BlockSpec(memory_space=pltpu.VMEM)
     sems = [2, 1, 2]
-    sems += [N_LEFT] * 3 + [N_RIGHT] * 4 + [N_PLUS] * 2 + [N_RIGHT] * 2
+    sems += [N_LEFT] * 3 + [N_RIGHT] * 4 + [N_PLUS] * 2 + [N_RIGHT] * 3
     sems += [N_LEFT] * 3 + [N_RIGHT] * 3 + [N_PLUS] * 2 + [N_RIGHT]
     scratch = [pltpu.VMEM((BLOCKS, *tail), dtype)] * 8 + [pltpu.VMEM((PLUS, *tail), dtype)] * 2
     scratch += [

time: 135 us -> 107 us (0.79)
  Pallas kernels: 135 us -> 105 us
    pallas_call x1, Pallas kernels: 126 us -> 97.3 us  [gather(): pl.pallas_call(gather_kernel, out_shape=[jax.ShapeDtypeStruct((PRODUCTS +...]
where the time goes in v1:
time: 107 us; the launch traced here: 105 us
  Pallas kernels  105 us (98%)
    pallas_call x1, Pallas kernels, gather(): pl.pallas_call(gather_kernel, out_shape=[jax.ShapeDtypeStruct((PRODUCTS +...  97.3 us
    pallas_call x1, Pallas kernels, on_device(): pl.pallas_call(place_kernel, out_shape=jax.ShapeDtypeStruct((1, 1, slots,...  8.07 us

profile of v1, /device:TPU:30, one launch (start us, length us, event | category | flops | bytes accessed | tf_op | source)
XLA Modules:
  0.0 105.4 jit_solution(8166776628367833896)
XLA Ops:
  0.0 97.3 %gather.1 = (bf16[136,256,256]{2,1,0:T(8,128)(2,1)}, s32[1,64]{1,0:T(1,128)}) custom-call(bf16[1,1,16,256,256]{4,3,2,1,0:T(8,128)(2,1)} %a_ref.1, bf16[1,1,16,256,256]{4,3,2,1,0:T(8,128)(2,1)} %b_ref.1, s32[16,16,16]{2,1,0:T(8,128)} %rows_ref.1, s32[16,16,16]{2,1,0:T(8,128)} %inner_ref.1, s32[16,16,16]{2,1,0:T(8,128)} %b_inner_ref.1, ...), custom_call_target="tpu_custom_call" | custom-call | tf_op jit(solution)/shard_map/gather/pallas_call | solution.py:487
  97.4 8.1 %place.1 = bf16[1,1,64,256,256]{4,3,2,1,0:T(8,128)(2,1)} custom-call(s32[1,64]{1,0:T(1,128)} %get-tuple-element.7.last, bf16[136,256,256]{2,1,0:T(8,128)(2,1)} %get-tuple-element.8.partial), custom_call_target="tpu_custom_call" | custom-call | tf_op jit(solution)/shard_map/place/pallas_call | solution.py:528

commit v2 on v1

--- a/solution.py
+++ b/solution.py
@@ -29,26 +29,29 @@
     return (x_lo * 8 + y * 2 + core, z * 2 + x_hi)
 
 
-LEAD = 1
-CROSS_AT = (-1, -1, -1, 3)
+LEAD = 2
+CROSS_AT = (-1, -1, -1, 1)
 HALF = N_RIGHT // 2
 RUN = 2
 RUNS = BLOCKS // RUN
 GROUP = 2 * RUN
 PRODUCTS = 2 * STEPS * BLOCKS
 NONE = PRODUCTS
-PIECES = ((0, 0, RUNS), (1, 0, 6), (3, 0, 2), (2, 0, 6), (3, 4, 1), (3, 3, 1), (3, 2, 1), (2, 6, 1), (2, 7, 1), (3, 5, 1), (1, 6, 1), (1, 7, 1), (3, 6, 1), (3, 7, 1))
+PIECES = ((0, 0, RUNS), (1, 0, 6), (2, 0, 6), (3, 3, 1), (2, 7, 1), (3, 0, 2), (3, 4, 1), (3, 2, 1), (3, 5, 1), (1, 6, 1), (2, 6, 1), (1, 7, 1), (3, 7, 1), (3, 6, 1))
 ORDERS = (
 (
-    ("rl", 0), ("j2", 0), ("rl", 4), ("j1", 0), ("q3", 0), ("rl", 5), ("j2", 1), ("q3", 1), ("rl", 1), ("rl", 7),
-    ("rl", 6), ("j2", 2), ("q3", 2), ("j1", 2), ("j2", 3), ("rl", 2), ("i2", 0), ("rl", 3), ("j2", 4), ("j1", 1),
-    ("i2", 1), ("j2", 5), ("i3", 0), ("i1", 0), ("j2", 6), ("j1", 3), ("i2", 5), ("i2", 4), ("i3", 1), ("i1", 1),
-    ("i3", 4), ("i1", 4), ("q6", 1), ("q6", 0), ("j1", 4), ("q6", 2), ("i2", 6), ("i3", 5), ("i1", 5), ("j2", 8),
-    ("j3", 1), ("i2", 7), ("i2", 2), ("i3", 2), ("i1", 2), ("j2", 7), ("i3", 6), ("i1", 6), ("i2", 3), ("j3", 0),
-    ("i3", 7), ("i1", 7), ("j2", 9), ("j1", 5), ("j1", 6), ("j3", 2), ("i3", 3), ("i1", 3), ("j3", 3), ("j3", 4),
-    ("j1", 7), ("j3", 7), ("j3", 5), ("j1", 8), ("j3", 8), ("j3", 6), ("j1", 9), ("j3", 9),
+    ("rl", 0), ("rl", 4), ("j2", 0), ("j1", 0), ("rl", 1), ("q3", 0), ("j2", 1), ("rl", 5), ("rl", 6), ("j1", 1),
+    ("j2", 2), ("q3", 1), ("j2", 3), ("rl", 2), ("q3", 2), ("rl", 3), ("j2", 4), ("j1", 2), ("rl", 7), ("i2", 0),
+    ("i3", 0), ("i1", 0), ("j2", 5), ("j2", 6), ("i2", 1), ("i3", 1), ("i1", 1), ("j3", 0), ("q6", 0), ("i2", 5),
+    ("j1", 3), ("i2", 2), ("q6", 1), ("i2", 6), ("i3", 5), ("i1", 5), ("j3", 1), ("i2", 4), ("j1", 4), ("i3", 2),
+    ("i1", 2), ("i3", 4), ("i1", 4), ("i3", 6), ("i1", 6), ("j2", 7), ("i2", 7), ("j1", 5), ("i2", 3), ("i3", 3),
+    ("i1", 3), ("q6", 2), ("j2", 8), ("i3", 7), ("i1", 7), ("j1", 6), ("j2", 9), ("j3", 4), ("j3", 2), ("j3", 3),
+    ("j1", 7), ("j3", 7), ("j3", 5), ("j1", 9), ("j1", 8), ("j3", 9), ("j3", 8), ("j3", 6),
 ),
 )
+
+
+EARLY = sum(count for _, _, count in PIECES[:2]) * GROUP
 
 
 def order_table():
@@ -108,7 +111,7 @@
 
 
 def gather_kernel(a_ref, b_ref, rows_ref, inner_ref, b_inner_ref, cols_ref, c_rows_ref, c_cols_ref, rank_row, rank_col,
-                  partial, last,
+                  partial, recent, last,
                   a_own, b_own, j1, j2, j3, i1, i2, i3, q3, q6, relay, sums, stage, table, plain,
                   own_sem, table_sem, stage_sem,
                   s_j1, s_j2, s_j3, s_i1, s_i2, s_i2b, s_i3, s_q3, s_q6, s_rl, s_fw, s_x,
@@ -254,7 +257,8 @@
         )
 
     for n in range(2):
-        put(PRODUCTS // GROUP + n).start()
+        put(EARLY // GROUP + n).start()
+    recent[PRODUCTS - EARLY] = jnp.zeros(recent.shape[1:], recent.dtype)
     to_plain.wait()
 
     def on_j2(k):
@@ -352,8 +356,9 @@
 
     lefts, rights = (a_own, j1, j2, j3), (b_own, i1, i2, i3)
 
-    def multiply_run(step, run, group):
-        put(group).wait()
+    def multiply_run(step, run, group, early):
+        if early:
+            put(group).wait()
         for n in range(RUN):
             block = lefts[step][run * RUN + n]
             for t in range(2):
@@ -363,17 +368,22 @@
                     block, rights[step][plain[0, j]], preferred_element_type=jnp.float32
                 )
                 sums[rank] = total
-                stage[group % 2, 2 * n + t] = total.astype(stage.dtype)
-        put(group).start()
+                if early:
+                    stage[group % 2, 2 * n + t] = total.astype(stage.dtype)
+                else:
+                    recent[rank - EARLY] = total.astype(recent.dtype)
+        if early:
+            put(group).start()
 
     def multiply(step, first, count, group):
+        early = group * GROUP < EARLY
         if count == 1:
-            multiply_run(step, first, group)
+            multiply_run(step, first, group, early)
         else:
 
             @pl.loop(0, count)
             def _(n):
-                multiply_run(step, first + n, group + n)
+                multiply_run(step, first + n, group + n, early)
 
     handlers = {
         "j1": on_j1, "j2": on_j2, "j3": on_j3, "q3": on_q3, "q6": on_q6,
@@ -487,42 +497,55 @@
     return pl.pallas_call(
         gather_kernel,
         out_shape=[
-            jax.ShapeDtypeStruct((PRODUCTS + 2 * GROUP, *tail), dtype),
+            jax.ShapeDtypeStruct((EARLY + 2 * GROUP + PRODUCTS, *tail), dtype),
+            pltpu.VMEM((PRODUCTS - EARLY + 1, *tail), dtype),
             jax.ShapeDtypeStruct((1, slots), jnp.int32),
         ],
         in_specs=[anywhere] * 2 + [in_vmem] * 8,
-        out_specs=[anywhere, in_vmem],
+        out_specs=[pl.BlockSpec(memory_space=pltpu.HBM), in_vmem, in_vmem],
         scratch_shapes=scratch + [pltpu.SemaphoreType.DMA((n,)) if n > 1 else pltpu.SemaphoreType.DMA for n in sems],
-        compiler_params=pltpu.CompilerParams(collective_id=0, has_side_effects=True, vmem_limit_bytes=67000000),
+        compiler_params=pltpu.CompilerParams(collective_id=0, has_side_effects=True, vmem_limit_bytes=57000000),
         name="gather",
     )(a_panels, b_panels, *indices, jnp.asarray(rank)[None, :], jnp.asarray(rank)[:, None])
 
 
-def place_kernel(last, partial, out, stage, in_sem, out_sem):
+def place_kernel(last, partial, recent, out, stage, in_sem, out_sem):
     count = stage.shape[0]
 
-    def fetch(n):
-        return pltpu.make_async_copy(partial.at[last[0, n]], stage.at[n], in_sem.at[n])
-
-    def put(n):
-        return pltpu.make_async_copy(stage.at[n], out.at[0, 0, n], out_sem.at[n])
+    def fetch(n, rank):
+        return pltpu.make_async_copy(partial.at[rank], stage.at[n], in_sem.at[n])
+
+    def put(n, src):
+        return pltpu.make_async_copy(src, out.at[0, 0, n], out_sem.at[n])
 
     @pl.loop(0, count)
     def _(n):
-        fetch(n).start()
+        rank = last[0, n]
+
+        @pl.when(rank < EARLY)
+        def _():
+            fetch(n, rank).start()
+
+        @pl.when(rank >= EARLY)
+        def _():
+            put(n, recent.at[rank - EARLY]).start()
 
     @pl.loop(0, count)
     def _(n):
-        fetch(n).wait()
-        put(n).start()
+        rank = last[0, n]
+
+        @pl.when(rank < EARLY)
+        def _():
+            fetch(n, rank).wait()
+            put(n, stage.at[n]).start()
 
     @pl.loop(0, count)
     def _(n):
-        put(n).wait()
+        put(n, stage.at[n]).wait()
 
 
 def on_device(a_panels, b_panels, a_rows, a_inner, b_inner, b_cols, c_rows, c_cols):
-    partial, last = gather(a_panels, b_panels, (a_rows, a_inner, b_inner, b_cols, c_rows, c_cols))
+    partial, recent, last = gather(a_panels, b_panels, (a_rows, a_inner, b_inner, b_cols, c_rows, c_cols))
     slots, width = c_rows.shape[2], a_panels.shape[3]
     anywhere = pl.BlockSpec(memory_space=pl.ANY)
     return pl.pallas_call(
@@ -531,7 +554,7 @@
         grid_spec=pltpu.PrefetchScalarGridSpec(
             num_scalar_prefetch=1,
             grid=(),
-            in_specs=[anywhere],
+            in_specs=[pl.BlockSpec(memory_space=pltpu.HBM), anywhere],
             out_specs=anywhere,
             scratch_shapes=[
                 pltpu.VMEM((slots, width, width), a_panels.dtype),
@@ -539,8 +562,9 @@
                 pltpu.SemaphoreType.DMA((slots,)),
             ],
         ),
+        compiler_params=pltpu.CompilerParams(vmem_limit_bytes=38000000),
         name="place",
-    )(last, partial)
+    )(last, partial, recent)
 
 
 def solution(mesh):

time: 107 us -> 102 us (0.953); the launches traced: 105 us -> 102 us
  Pallas kernels: 105 us -> 102 us
    pallas_call x1, Pallas kernels: 8.07 us -> 5.55 us  [on_device(): pl.pallas_call(place_kernel, out_shape=jax.ShapeDtypeStruct((1, 1, slots,...]
    pallas_call x1, Pallas kernels: 97.3 us -> 96 us  [gather(): pl.pallas_call(gather_kernel, out_shape=[jax.ShapeDtypeStruct((EARLY + 2...]
where the time goes in v2:
time: 102 us
  Pallas kernels  102 us (100%)
    pallas_call x1, Pallas kernels, gather(): pl.pallas_call(gather_kernel, out_shape=[jax.ShapeDtypeStruct((EARLY + 2...  96 us
    pallas_call x1, Pallas kernels, on_device(): pl.pallas_call(place_kernel, out_shape=jax.ShapeDtypeStruct((1, 1, slots,...  5.55 us

profile of v2, /device:TPU:30, one launch (start us, length us, event | category | flops | bytes accessed | tf_op | source)
XLA Modules:
  0.0 102.2 jit_solution(12378662383057722036)
XLA Ops:
  0.0 96.0 %gather.1 = (bf16[192,256,256]{2,1,0:T(8,128)(2,1)}, bf16[73,256,256]{2,1,0:T(8,128)(2,1)S(1)}, s32[1,64]{1,0:T(1,128)}) custom-call(bf16[1,1,16,256,256]{4,3,2,1,0:T(8,128)(2,1)} %a_ref.1, bf16[1,1,16,256,256]{4,3,2,1,0:T(8,128)(2,1)} %b_ref.1, s32[16,16,16]{2,1,0:T(8,128)} %rows_ref.1, s32[16,16,16]{2,1,0:T(8,128)} %inner_ref.1, ...), custom_call_target="tpu_custom_call" | custom-call | tf_op jit(solution)/shard_map/gather/pallas_call | solution.py:497
  96.0 0.0 copy-start
  96.0 0.6 copy-done
  96.6 5.6 %place.1 = bf16[1,1,64,256,256]{4,3,2,1,0:T(8,128)(2,1)} custom-call(s32[1,64]{1,0:T(1,128)S(1)} %copy-done, bf16[192,256,256]{2,1,0:T(8,128)(2,1)} %get-tuple-element.9.partial, bf16[73,256,256]{2,1,0:T(8,128)(2,1)S(1)} %get-tuple-element.10.recent), custom_call_target="tpu_custom_call" | custom-call | tf_op jit(solution)/shard_map/place/pallas_call | solution.py:551
Async XLA Ops:
  96.0 0.6 copy-start

commit v3 on v2

--- a/solution.py
+++ b/solution.py
@@ -518,7 +518,7 @@
     def put(n, src):
         return pltpu.make_async_copy(src, out.at[0, 0, n], out_sem.at[n])
 
-    @pl.loop(0, count)
+    @pl.loop(0, count, unroll=8)
     def _(n):
         rank = last[0, n]
 
@@ -526,20 +526,24 @@
         def _():
             fetch(n, rank).start()
 
-        @pl.when(rank >= EARLY)
-        def _():
-            put(n, recent.at[rank - EARLY]).start()
-
-    @pl.loop(0, count)
+    @pl.loop(0, count, unroll=8)
     def _(n):
         rank = last[0, n]
 
+        @pl.when(rank >= EARLY)
+        def _():
+            put(n, recent.at[rank - EARLY]).start()
+
+    @pl.loop(0, count, unroll=8)
+    def _(n):
+        rank = last[0, n]
+
         @pl.when(rank < EARLY)
         def _():
             fetch(n, rank).wait()
             put(n, stage.at[n]).start()
 
-    @pl.loop(0, count)
+    @pl.loop(0, count, unroll=8)
     def _(n):
         put(n, stage.at[n]).wait()
 

time: 102 us -> 102 us (level)
  no operation moved by 1% of the time
where the time goes in v3:
time: 102 us
  Pallas kernels  101 us (99%)
    pallas_call x1, Pallas kernels, gather(): pl.pallas_call(gather_kernel, out_shape=[jax.ShapeDtypeStruct((EARLY + 2...  96 us
    pallas_call x1, Pallas kernels, on_device(): pl.pallas_call(place_kernel, out_shape=jax.ShapeDtypeStruct((1, 1, slots,...  5.11 us

profile of v3, /device:TPU:30, one launch (start us, length us, event | category | flops | bytes accessed | tf_op | source)
XLA Modules:
  0.0 101.7 jit_solution(4728757175353385275)
XLA Ops:
  0.0 96.0 %gather.1 = (bf16[192,256,256]{2,1,0:T(8,128)(2,1)}, bf16[73,256,256]{2,1,0:T(8,128)(2,1)S(1)}, s32[1,64]{1,0:T(1,128)}) custom-call(bf16[1,1,16,256,256]{4,3,2,1,0:T(8,128)(2,1)} %a_ref.1, bf16[1,1,16,256,256]{4,3,2,1,0:T(8,128)(2,1)} %b_ref.1, s32[16,16,16]{2,1,0:T(8,128)} %rows_ref.1, s32[16,16,16]{2,1,0:T(8,128)} %inner_ref.1, ...), custom_call_target="tpu_custom_call" | custom-call | tf_op jit(solution)/shard_map/gather/pallas_call | solution.py:497
  96.0 0.0 copy-start
  96.0 0.6 copy-done
  96.6 5.1 %place.1 = bf16[1,1,64,256,256]{4,3,2,1,0:T(8,128)(2,1)} custom-call(s32[1,64]{1,0:T(1,128)S(1)} %copy-done, bf16[192,256,256]{2,1,0:T(8,128)(2,1)} %get-tuple-element.9.partial, bf16[73,256,256]{2,1,0:T(8,128)(2,1)S(1)} %get-tuple-element.10.recent), custom_call_target="tpu_custom_call" | custom-call | tf_op jit(solution)/shard_map/place/pallas_call | solution.py:555
Async XLA Ops:
  96.0 0.6 copy-start
